TPU v7x, 32 devices: a whole 2x2x4 slice. The times are simulated.
32 devices in a mesh: space: 8 (over y, x, core), chan: 4 (over z).
Axes of the slice: x: 2, y: 2, z: 4, core: 2. Of those that a mesh axis runs over, the one named last changes fastest.
Arguments:
- points: bfloat16 [256, 8, 16384], P('chan', 'space'), may hold values from -6 to 6
- point_cell: int32 [8, 16384], P('space'), may hold values from 0 to 4096, as said below
- conv_weight: bfloat16 [27, 256, 256], P(None, 'chan'), may hold values from -0.109375 to 0.109375
- conv_bias: bfloat16 [256], P('chan'), may hold values from -3 to 3
- neighbors: int32 [64, 27], P('space'), may hold values from -1 to 23, as said below
Outputs:
- voxel_out: bfloat16 [256, 32768], P('chan', 'space')
- point_out: bfloat16 [256, 8, 16384], P('chan', 'space')
Inputs may be any that keep to these rules, and one draw needn't show every extreme that they name: `point_cell`: in each aligned block of 2048 slots from one sender the live slots (cell below 4096) come first; in every draw some owner receives 2048 live slots from every sender. `neighbors`: entry 13 is the block's own slot 8 + b; blocks of one owner lie on a 4 x (4) grid of a strip, strips of owners d and d+1 adjacent.
All inputs are finite; a program needn't handle non-finite values.
Results may differ from a plain program's by a relative error of at most 0.01.
Values may be sent and summed in bfloat16 or wider, within the bound.
A program may use at most 128 MiB of HBM per device.

v0:
```python
import jax
import jax.numpy as jnp
import numpy as np
from jax import lax
from jax.sharding import PartitionSpec as P


def extended_2(cells, sides, width):
    for axis, dim in sides:
        count = lax.axis_size(axis)
        ends = count - 1
        head = lax.slice_in_dim(cells, 0, width, axis=dim)
        tail = lax.slice_in_dim(cells, cells.shape[dim] - width, cells.shape[dim], axis=dim)
        cells = jnp.concatenate(
            [
                lax.ppermute(tail, axis, [(i, (i + 1) % count) for i in range(ends)]),
                cells,
                lax.ppermute(head, axis, [((i + 1) % count, i) for i in range(ends)]),
            ],
            axis=dim,
        )
    return cells


def reach_tables(coord_x, coord_y, coord_z):

    def split_axis(values):
        moved = np.where(values < 0, -1, np.where(values > 7, 1, 0))
        return (moved, values - 8 * moved)

    move_x, inner_x = split_axis(coord_x)
    move_y, inner_y = split_axis(coord_y)
    move_z, inner_z = split_axis(coord_z)
    direction = 9 * (move_x + 1) + 3 * (move_y + 1) + (move_z + 1)
    inner = 64 * inner_x + 8 * inner_y + inner_z
    return (direction.astype(np.int32), inner.astype(np.int32))


def margin_tables():
    spots = np.arange(1000)
    return reach_tables(spots // 100 - 1, spots // 10 % 10 - 1, spots % 10 - 1)


def window_table():
    cells = np.arange(512)
    base = cells // 64 * 100 + cells // 8 % 8 * 10 + cells % 8
    shifts = np.arange(27)
    step = shifts // 9 * 100 + shifts // 3 % 3 * 10 + shifts % 3
    return (step[:, None] + base[None, :]).astype(np.int32)


def source_index(neighbors, direction, inner, spare):
    slots = jnp.take(neighbors, jnp.asarray(direction), axis=1)
    slots = jnp.where(slots < 0, spare, slots)
    return slots * 512 + jnp.asarray(inner)[None]


def pool_blocks(features, cell_ids, block_count):
    row_total = features.shape[1]
    step_rows = min(row_total, 2048)
    turns = row_total // step_rows
    targets = jnp.arange(block_count * 512, dtype=jnp.int32)
    width_here = features.shape[0]

    def accumulate(turn, carry):
        summed, tallies = carry
        rows = lax.dynamic_slice_in_dim(features, turn * step_rows, step_rows, 1)
        ids = lax.dynamic_slice_in_dim(cell_ids, turn * step_rows, step_rows, 0)
        onehot = (ids[:, None] == targets[None, :]).astype(jnp.bfloat16)
        summed = summed + jnp.dot(rows, onehot, preferred_element_type=jnp.float32)
        tallies = tallies + jnp.sum(onehot, axis=0, dtype=jnp.float32)
        return (summed, tallies)

    start = (
        jnp.zeros((width_here, block_count * 512), jnp.float32),
        jnp.zeros((block_count * 512,), jnp.float32),
    )
    summed, tallies = lax.fori_loop(0, turns, accumulate, start)
    voxels = (summed / jnp.maximum(tallies, 1.0)[None, :]).astype(jnp.bfloat16)
    return (voxels.reshape(width_here, block_count, 512), tallies)


def on_device(points, point_cell, conv_weight, conv_bias, neighbors):
    width_local = points.shape[0]
    owners = lax.axis_size("space")
    slot_total = points.shape[2]
    slot_cap = slot_total // owners
    block_count = neighbors.shape[0]
    arrived = lax.all_to_all(points, "space", split_axis=2, concat_axis=1, tiled=True)
    features = arrived.reshape(width_local, owners * slot_cap)
    cell_ids = point_cell[0]
    voxels, tallies = pool_blocks(features, cell_ids, block_count)
    active = jnp.where(tallies > 0.0, 1.0, 0.0).astype(jnp.float32)
    source = extended_2(voxels, (("space", 1),), block_count)
    source = jnp.concatenate([source, jnp.zeros((width_local, 1, 512), jnp.bfloat16)], 1)
    flat_source = source.reshape(width_local, (3 * block_count + 1) * 512)
    spare = 3 * block_count
    weight_all, bias_all = (
        lax.all_gather(conv_weight, "chan", axis=1, tiled=True),
        lax.all_gather(conv_bias, "chan", axis=0, tiled=True),
    )
    groups = lax.axis_size("chan")
    share = block_count // groups
    margin_dir, margin_inner = margin_tables()
    margin_index = source_index(neighbors, margin_dir, margin_inner, spare).reshape(
        block_count * 1000
    )
    margins = jnp.take(flat_source, margin_index, axis=1).reshape(width_local, block_count, 1000)
    spread = lax.all_to_all(margins, "chan", split_axis=1, concat_axis=0, tiled=True)
    width_all = spread.shape[0]
    flat_spread = spread.reshape(width_all, share * 1000)
    window = jnp.asarray(window_table())
    block_base = (jnp.arange(share, dtype=jnp.int32) * 1000)[None, :, None]
    column_index = (block_base + window[:, None, :]).reshape(27, share * 512)
    stacked = jnp.take(flat_spread, column_index, axis=1)
    total = jnp.zeros((width_all, share * 512), jnp.float32)
    for group in range(groups):
        low = group * width_local
        partial_sum = jnp.einsum(
            "ion,oic->cn",
            stacked[low : low + width_local],
            weight_all[:, low : low + width_local, :],
            preferred_element_type=jnp.float32,
        ).astype(jnp.bfloat16)
        partial_sum = lax.optimization_barrier(partial_sum)
        total = total + partial_sum.astype(jnp.float32)
    mine = lax.dynamic_slice_in_dim(active, lax.axis_index("chan") * (share * 512), share * 512, 0)
    finished = (
        jnp.maximum(total + bias_all.astype(jnp.float32)[:, None], 0.0) * mine[None, :]
    ).astype(jnp.bfloat16)
    voxel_out = lax.all_to_all(finished, "chan", split_axis=0, concat_axis=1, tiled=True)
    extended = jnp.concatenate([voxel_out, jnp.zeros((width_local, 1), jnp.bfloat16)], 1)
    picked = jnp.take(extended, cell_ids, axis=1).reshape(width_local, owners, slot_cap)
    returned = lax.all_to_all(picked, "space", split_axis=1, concat_axis=2, tiled=True)
    point_out = (points.astype(jnp.float32) + returned.astype(jnp.float32)).astype(jnp.bfloat16)
    return (voxel_out, point_out)


def solution(mesh):
    return jax.shard_map(
        on_device,
        mesh=mesh,
        in_specs=(
            P("chan", "space", None),
            P("space", None),
            P(None, "chan", None),
            P("chan"),
            P("space", None),
        ),
        out_specs=(P("chan", "space"), P("chan", "space", None)),
        check_vma=False,
    )
```

profile of v0, /device:TPU:0, one launch (start us, length us, event | category | flops | bytes accessed | tf_op | source)
XLA Modules:
  0.0 661.8 jit_solution(425877067838428987)
XLA Ops:
  7.2 17.2 %copy.80 = bf16[64,1,16384]{0,1,2:T(2,128)(2,1)} copy(bf16[64,1,16384]{2,0,1:T(8,128)(2,1)} %param.10) | data formatting | bytes 4194304 | tf_op args[0]
  24.9 90.8 %reduce.6 = bf16[16384,64]{1,0:T(8,128)(2,1)} reduce(bf16[16384,1,64]{2,1,0:T(2,128)(2,1)} %bitcast.73, bf16[]{:T(256)} %broadcast.224), dimensions={1}, to_apply=%bitcast.69.reduce_sub_computation | reduce | bytes 4194306
  115.6 7.6 %reshape.286 = bf16[8,2,65536]{2,1,0:T(2,128)(2,1)} reshape(bf16[16384,64]{1,0:T(8,128)(2,1)} %reduce.6) | data formatting | bytes 4194304
  123.2 5.3 all-to-all-start
  129.4 2.9 gather_fusion
  132.9 22.3 %all-to-all-done = bf16[8,2,65536]{2,1,0:T(2,128)(2,1)S(1)} async-done(((bf16[8,2,65536]{2,1,0:T(2,128)(2,1)}), bf16[8,2,65536]{2,1,0:T(2,128)(2,1)S(1)}, u32[]{:S(2)}, u32[]{:S(2)}) %all-to-all-start) | async-done | bytes 2097184 | tf_op jit(solution)/shard_map/all_to_all | solution.py:89
  155.2 5.9 reshape.287
  161.0 15.5 %copy.81 = bf16[64,1,16384]{2,0,1:T(8,128)(2,1)S(1)} copy(bf16[64,1,16384]{0,1,2:T(2,128)(2,1)} %bitcast.74) | data formatting | bytes 4194304 | tf_op jit(solution)/shard_map/all_to_all | solution.py:89
  176.6 115.7 %while.16 = (s32[]{:T(128)}, f32[64,4096]{1,0:T(8,128)}, f32[4096]{0:T(1024)S(1)}, bf16[64,16384]{1,0:T(8,128)(2,1)S(1)}, s32[16384]{0:T(1024)S(1)}, /*index=5*/s32[]{:T(128)}, s32[]{:T(128)}, s32[]{:T(128)}, s32[]{:T(128)}) while((s32[]{:T(128)}, f32[64,4096]{1,0:T(8,128)}, f32[4096]{0:T(1024)S(1)}, ...), condition=%wide.region_2.0_spmd.clone, body=%wide.region_0.0_spmd.clone.sunk | while | flops 1116213248 | bytes 2457758 | solution.py:78
  176.8 8.0 %fusion.65 = f32[64,4096]{1,0:T(8,128)} fusion(s32[2048]{0:T(1024)S(1)} %dynamic_slice.29, f32[64,4096]{1,0:T(8,128)} %get-tuple-element.202, pred[]{:T(512)S(6)} %compare.4, bf16[64,16384]{1,0:T(8,128)(2,1)S(1)} %get-tuple-element.213, s32[]{:T(128)S(6)} %select_n.172), kind=kOutput, calls=%fused_computation.10.clone.1 | convolution fusion | flops 1082654720 | bytes 2367493 | tf_op jit(solution)/shard_map/while/body/eval_jaxpr/dot_general | solution.py:70
  184.8 5.3 convert_reduce_fusion.2
  190.1 9.2 %fusion.65 = f32[64,4096]{1,0:T(8,128)} fusion(s32[2048]{0:T(1024)S(1)} %dynamic_slice.29, f32[64,4096]{1,0:T(8,128)} %get-tuple-element.202, pred[]{:T(512)S(6)} %compare.4, bf16[64,16384]{1,0:T(8,128)(2,1)S(1)} %get-tuple-element.213, s32[]{:T(128)S(6)} %select_n.172), kind=kOutput, calls=%fused_computation.10.clone.1 | convolution fusion | flops 1082654720 | bytes 2367493 | tf_op jit(solution)/shard_map/while/body/eval_jaxpr/dot_general | solution.py:70
  199.4 5.3 convert_reduce_fusion.2
  204.7 9.2 %fusion.65 = f32[64,4096]{1,0:T(8,128)} fusion(s32[2048]{0:T(1024)S(1)} %dynamic_slice.29, f32[64,4096]{1,0:T(8,128)} %get-tuple-element.202, pred[]{:T(512)S(6)} %compare.4, bf16[64,16384]{1,0:T(8,128)(2,1)S(1)} %get-tuple-element.213, s32[]{:T(128)S(6)} %select_n.172), kind=kOutput, calls=%fused_computation.10.clone.1 | convolution fusion | flops 1082654720 | bytes 2367493 | tf_op jit(solution)/shard_map/while/body/eval_jaxpr/dot_general | solution.py:70
  213.9 5.3 convert_reduce_fusion.2
  219.3 9.2 %fusion.65 = f32[64,4096]{1,0:T(8,128)} fusion(s32[2048]{0:T(1024)S(1)} %dynamic_slice.29, f32[64,4096]{1,0:T(8,128)} %get-tuple-element.202, pred[]{:T(512)S(6)} %compare.4, bf16[64,16384]{1,0:T(8,128)(2,1)S(1)} %get-tuple-element.213, s32[]{:T(128)S(6)} %select_n.172), kind=kOutput, calls=%fused_computation.10.clone.1 | convolution fusion | flops 1082654720 | bytes 2367493 | tf_op jit(solution)/shard_map/while/body/eval_jaxpr/dot_general | solution.py:70
  228.5 5.3 convert_reduce_fusion.2
  233.8 9.2 %fusion.65 = f32[64,4096]{1,0:T(8,128)} fusion(s32[2048]{0:T(1024)S(1)} %dynamic_slice.29, f32[64,4096]{1,0:T(8,128)} %get-tuple-element.202, pred[]{:T(512)S(6)} %compare.4, bf16[64,16384]{1,0:T(8,128)(2,1)S(1)} %get-tuple-element.213, s32[]{:T(128)S(6)} %select_n.172), kind=kOutput, calls=%fused_computation.10.clone.1 | convolution fusion | flops 1082654720 | bytes 2367493 | tf_op jit(solution)/shard_map/while/body/eval_jaxpr/dot_general | solution.py:70
  243.1 5.3 convert_reduce_fusion.2
  248.4 9.2 %fusion.65 = f32[64,4096]{1,0:T(8,128)} fusion(s32[2048]{0:T(1024)S(1)} %dynamic_slice.29, f32[64,4096]{1,0:T(8,128)} %get-tuple-element.202, pred[]{:T(512)S(6)} %compare.4, bf16[64,16384]{1,0:T(8,128)(2,1)S(1)} %get-tuple-element.213, s32[]{:T(128)S(6)} %select_n.172), kind=kOutput, calls=%fused_computation.10.clone.1 | convolution fusion | flops 1082654720 | bytes 2367493 | tf_op jit(solution)/shard_map/while/body/eval_jaxpr/dot_general | solution.py:70
  257.6 5.3 convert_reduce_fusion.2
  263.0 9.2 %fusion.65 = f32[64,4096]{1,0:T(8,128)} fusion(s32[2048]{0:T(1024)S(1)} %dynamic_slice.29, f32[64,4096]{1,0:T(8,128)} %get-tuple-element.202, pred[]{:T(512)S(6)} %compare.4, bf16[64,16384]{1,0:T(8,128)(2,1)S(1)} %get-tuple-element.213, s32[]{:T(128)S(6)} %select_n.172), kind=kOutput, calls=%fused_computation.10.clone.1 | convolution fusion | flops 1082654720 | bytes 2367493 | tf_op jit(solution)/shard_map/while/body/eval_jaxpr/dot_general | solution.py:70
  272.2 5.3 convert_reduce_fusion.2
  277.5 9.2 %fusion.65 = f32[64,4096]{1,0:T(8,128)} fusion(s32[2048]{0:T(1024)S(1)} %dynamic_slice.29, f32[64,4096]{1,0:T(8,128)} %get-tuple-element.202, pred[]{:T(512)S(6)} %compare.4, bf16[64,16384]{1,0:T(8,128)(2,1)S(1)} %get-tuple-element.213, s32[]{:T(128)S(6)} %select_n.172), kind=kOutput, calls=%fused_computation.10.clone.1 | convolution fusion | flops 1082654720 | bytes 2367493 | tf_op jit(solution)/shard_map/while/body/eval_jaxpr/dot_general | solution.py:70
  286.8 5.3 convert_reduce_fusion.2
  297.1 2.5 collective-permute-done.1
  301.7 3.9 copy.82
  305.6 17.3 %gather_fusion.1 = bf16[8000,64]{1,0:T(8,128)(2,1)} fusion(bf16[64,12800]{0,1:T(8,128)(2,1)S(1)} %bitcast.72, s32[8192]{0:T(1024)S(1)} %pad_clamp_fusion), kind=kCustom, calls=%fused_computation.1 | custom fusion | bytes 2080000 | tf_op jit(solution)/shard_map/jit(_take)/gather | solution.py:108
  326.0 4.9 all-to-all-start.1
  332.8 13.9 %all-reduce.1 = bf16[256]{0:T(256)(128)(2,1)S(1)} all-reduce(bf16[256]{0:T(256)(128)(2,1)S(1)} %dynamic-update-slice), channel_id=1, replica_groups=mesh['space'=8,'chan'=4] {'chan'}, use_global_device_ids=true, to_apply=%add.1 | all-reduce | flops 256 | bytes 1024
  348.1 6.2 all-to-all-done.1
  355.2 3.8 copy.94
  360.4 109.4 %gather_fusion.2 = bf16[27648,256]{1,0:T(8,128)(2,1)} fusion(bf16[256,2000]{0,1:T(8,128)(2,1)S(1)} %reshape.274, s32[27648]{0:T(1024)S(1)} %broadcast_clamp_fusion), kind=kCustom, calls=%fused_computation.2 | custom fusion | bytes 28422144 | tf_op jit(solution)/shard_map/jit(_take)/gather | solution.py:115
  469.8 18.7 %copy.88 = bf16[27,1024,256]{1,2,0:T(8,128)(2,1)} copy(bf16[27,1024,256]{2,1,0:T(8,128)(2,1)} %bitcast.71) | data formatting | bytes 28311552 | tf_op jit(solution)/shard_map/jit(_take)/gather | solution.py:115
  488.4 12.6 %select_bitcast_fusion = bf16[256,27,1024]{2,0,1:T(8,128)(2,1)} fusion(bf16[27,1024,256]{1,2,0:T(8,128)(2,1)} %copy.88, pred[27,1024]{1,0:T(8,128)(4,1)S(1)} %compare_and_fusion.1), kind=kLoop, calls=%fused_computation.14 | loop fusion | flops 7077888 | bytes 28339200 | tf_op jit(solution)/shard_map/jit(_take)/select_n | solution.py:115
  501.0 3.6 fusion.40
  504.6 2.8 copy-done
  507.4 2.5 fusion.43
  513.7 7.4 %all-to-all-start.2 = ((bf16[4,64,1024]{2,1,0:T(8,128)(2,1)}), bf16[4,64,1024]{2,1,0:T(8,128)(2,1)S(1)}, u32[]{:S(2)}, u32[]{:S(2)}) async-start(bf16[4,64,1024]{2,1,0:T(8,128)(2,1)} %bitcast.19), calls=%async_computation.2 | async-start | bytes 1048576 | tf_op jit(solution)/shard_map/all_to_all | solution.py:131
  521.1 15.1 %all-to-all-done.2 = bf16[4,64,1024]{2,1,0:T(8,128)(2,1)S(1)} async-done(((bf16[4,64,1024]{2,1,0:T(8,128)(2,1)}), bf16[4,64,1024]{2,1,0:T(8,128)(2,1)S(1)}, u32[]{:S(2)}, u32[]{:S(2)}) %all-to-all-start.2) | async-done | bytes 524320 | tf_op jit(solution)/shard_map/all_to_all | solution.py:131
  537.0 57.8 %gather_fusion.3 = bf16[16384,64]{1,0:T(8,128)(2,1)} fusion(bf16[64,4097]{0,1:T(8,128)(2,1)S(1)} %concatenate.7, s32[16384]{0:T(1024)S(1)} %broadcast_clamp_fusion.1), kind=kCustom, calls=%fused_computation.3 | custom fusion | bytes 4259840 | tf_op jit(solution)/shard_map/jit(_take)/gather | solution.py:133
  594.7 4.8 copy.91
  599.5 3.1 broadcast_select_fusion
  602.6 11.8 %all-to-all-start.3 = ((bf16[64,8,2048]{2,0,1:T(8,128)(2,1)}), bf16[64,8,2048]{2,0,1:T(8,128)(2,1)}, u32[]{:S(2)}, u32[]{:S(2)}) async-start(bf16[64,8,2048]{2,0,1:T(8,128)(2,1)} %broadcast_select_fusion), calls=%async_computation.3 | async-start | bytes 4194304 | tf_op jit(solution)/shard_map/all_to_all | solution.py:134
  615.6 25.6 %all-to-all-done.3 = bf16[64,8,2048]{2,0,1:T(8,128)(2,1)} async-done(((bf16[64,8,2048]{2,0,1:T(8,128)(2,1)}), bf16[64,8,2048]{2,0,1:T(8,128)(2,1)}, u32[]{:S(2)}, u32[]{:S(2)}) %all-to-all-start.3) | async-done | bytes 2097184 | tf_op jit(solution)/shard_map/all_to_all | solution.py:134
  641.2 4.8 copy.92
  646.0 5.1 reshape.231
  651.1 3.9 add_convert_fusion
  (93 shorter events, 22.3 us)
Async XLA Ops:
  123.2 6.1 copy-start.6
  123.2 6.2 copy-start.7
  123.2 9.4 %copy-start.5 = (s32[1000]{0:T(1024)S(1)}, s32[1000]{0:T(1024)}, u32[]{:S(2)}) copy-start(s32[1000]{0:T(1024)} %constant.126.clone) | copy-start | bytes 12004
  123.2 9.5 %copy-start.3 = (s32[1,16384]{1,0:T(1,128)S(1)}, s32[1,16384]{1,0:T(1,128)}, u32[]{:S(2)}) copy-start(s32[1,16384]{1,0:T(1,128)} %param.11) | copy-start | bytes 196612
  123.2 32.0 %all-to-all-start = ((bf16[8,2,65536]{2,1,0:T(2,128)(2,1)}), bf16[8,2,65536]{2,1,0:T(2,128)(2,1)S(1)}, u32[]{:S(2)}, u32[]{:S(2)}) async-start(bf16[8,2,65536]{2,1,0:T(2,128)(2,1)} %reshape.286), calls=%async_computation | async-start | bytes 4194304 | tf_op jit(solution)/shard_map/all_to_all | solution.py:89
  128.6 372.5 %all-gather.2.cloned.1.call-start = ((), (), s32[]{:S(2)}) async-start(), calls=%async_computation.4 | async-start | bytes 4423680 | tf_op jit(solution)/shard_map/all_gather | solution.py:99
  293.8 3.3 collective-permute-start
  295.1 4.5 collective-permute-start.1
  322.9 8.0 %copy-start.4 = (s32[27,512]{1,0:T(8,128)S(1)}, s32[27,512]{1,0:T(8,128)}, u32[]{:S(2)}) copy-start(s32[27,512]{1,0:T(8,128)} %constant.127.clone) | copy-start | bytes 165892
  324.9 6.4 copy-start.10
  324.9 7.6 %copy-start.9 = (bf16[64]{0:T(256)(128)(2,1)S(1)}, bf16[64]{0:T(256)(128)(2,1)}, u32[]{:S(2)}) copy-start(bf16[64]{0:T(256)(128)(2,1)} %param.13) | copy-start | bytes 388
  326.0 28.3 %all-to-all-start.1 = ((bf16[64,8,1000]{2,0,1:T(8,128)(2,1)}), bf16[64,8,1000]{2,0,1:T(8,128)(2,1)S(1)}, u32[]{:S(2)}, u32[]{:S(2)}) async-start(bf16[64,8,1000]{2,0,1:T(8,128)(2,1)} %broadcast_select_fusion.1), calls=%async_computation.1 | async-start | bytes 2097152 | tf_op jit(solution)/shard_map/all_to_all | solution.py:109
  354.3 1.0 copy-start.2
  501.0 6.4 copy-start
  507.4 2.5 copy-start.8
  513.7 22.6 %all-to-all-start.2 = ((bf16[4,64,1024]{2,1,0:T(8,128)(2,1)}), bf16[4,64,1024]{2,1,0:T(8,128)(2,1)S(1)}, u32[]{:S(2)}, u32[]{:S(2)}) async-start(bf16[4,64,1024]{2,1,0:T(8,128)(2,1)} %bitcast.19), calls=%async_computation.2 | async-start | bytes 1048576 | tf_op jit(solution)/shard_map/all_to_all | solution.py:131
  602.6 38.6 %all-to-all-start.3 = ((bf16[64,8,2048]{2,0,1:T(8,128)(2,1)}), bf16[64,8,2048]{2,0,1:T(8,128)(2,1)}, u32[]{:S(2)}, u32[]{:S(2)}) async-start(bf16[64,8,2048]{2,0,1:T(8,128)(2,1)} %broadcast_select_fusion), calls=%async_computation.3 | async-start | bytes 4194304 | tf_op jit(solution)/shard_map/all_to_all | solution.py:134
  646.0 5.1 copy-start.1
Sparse Core Ops, SparseCore 0:
  130.9 71.6 all-gather.1
where the time goes:
time: 665 us; the launch traced here: 662 us
  local copies, waits for them, and re-layouts  288 us (43%)
  other arithmetic  159 us (24%)
  matrix products  81 us (12%)
  waiting for transfers between devices  72.4 us (11%)
  starting transfers between devices  32.1 us (5%)
  between operations  15.1 us (2%)
  blocking collectives  13.9 us (2%)
    gather x2, local copies, waits for them, and re-layouts, on_device(): stacked = jnp.take(flat_spread, column_index, axis=1)  128 us
    unnamed x4, other arithmetic  91.6 us
    dot_general x8, matrix products, accumulate(): summed = summed + jnp.dot(rows, onehot, preferred_element_type=jnp.float32)  72.6 us
    gather x2, local copies, waits for them, and re-layouts, on_device(): jnp.take(extended, cell_ids, axis=1).reshape(width_local, owners, slot_cap)  62.5 us
    reduce_sum x8, other arithmetic, accumulate(): tallies = tallies + jnp.sum(onehot, axis=0, dtype=jnp.float32)  42.2 us
    unnamed x37, local copies, waits for them, and re-layouts  37.8 us
    all_to_all x1, waiting for transfers between devices, on_device(): lax.all_to_all(picked, 'space', split_axis=1, concat_axis=2, tiled=True)  25.6 us
    all_to_all x1, waiting for transfers between devices, on_device(): lax.all_to_all(points, 'space', split_axis=2, concat_axis=1, tiled=True)  22.3 us
  transfers between devices with their start and end apart: 7, of which 5 were waited for; matrix products, arithmetic and copies ran while one was open for 48% of the time, Pallas kernels for 0%

commit v1 on v0

--- a/solution.py
+++ b/solution.py
@@ -86,7 +86,19 @@
     slot_total = points.shape[2]
     slot_cap = slot_total // owners
     block_count = neighbors.shape[0]
-    arrived = lax.all_to_all(points, "space", split_axis=2, concat_axis=1, tiled=True)
+
+    def handle_the_sizes(here_x):
+        return jnp.concatenate(
+            jax.lax.all_to_all(
+                jnp.stack(jnp.split(here_x, jax.lax.axis_size("space"), axis=2), axis=0),
+                concat_axis=0,
+                split_axis=0,
+                axis_name="space",
+            ),
+            axis=1,
+        )
+
+    arrived = handle_the_sizes(points)
     features = arrived.reshape(width_local, owners * slot_cap)
     cell_ids = point_cell[0]
     voxels, tallies = pool_blocks(features, cell_ids, block_count)

time: 665 us -> 540 us (0.81)
  other arithmetic: 159 us -> 68.2 us
  local copies, waits for them, and re-layouts: 288 us -> 255 us
    unnamed x4 -> x3, other arithmetic: 91.6 us -> 0.8 us
    unnamed x37 -> x41, local copies, waits for them, and re-layouts: 37.8 us -> 19.9 us
    all_to_all x1 -> x0, local copies, waits for them, and re-layouts: 15.5 us -> none  [on_device(): lax.all_to_all(points, 'space', split_axis=2, concat_axis=1, tiled=True)]
  transfers between devices with their start and end apart: 7 -> 7, of which waited for: 5 -> 5; matrix products, arithmetic and copies ran while one was open for 48% -> 55% of each run, Pallas kernels for 0% -> 0%
where the time goes in v1:
time: 540 us; the launch traced here: 539 us
  local copies, waits for them, and re-layouts  255 us (47%)
  matrix products  81.9 us (15%)
  waiting for transfers between devices  72.4 us (13%)
  other arithmetic  68.2 us (13%)
  starting transfers between devices  31.8 us (6%)
  between operations  15.1 us (3%)
  blocking collectives  13.9 us (3%)
    gather x2, local copies, waits for them, and re-layouts, on_device(): stacked = jnp.take(flat_spread, column_index, axis=1)  127 us
    dot_general x8, matrix products, accumulate(): summed = summed + jnp.dot(rows, onehot, preferred_element_type=jnp.float32)  73.4 us
    gather x2, local copies, waits for them, and re-layouts, on_device(): jnp.take(extended, cell_ids, axis=1).reshape(width_local, owners, slot_cap)  62.2 us
    reduce_sum x8, other arithmetic, accumulate(): tallies = tallies + jnp.sum(onehot, axis=0, dtype=jnp.float32)  42.3 us
    all_to_all x1, waiting for transfers between devices, on_device(): lax.all_to_all(picked, 'space', split_axis=1, concat_axis=2, tiled=True)  25.6 us
    all_to_all x1, waiting for transfers between devices, handle_the_sizes(): jax.lax.all_to_all(jnp.stack(jnp.split(here_x, jax.lax.axis_size('space')...  22.3 us
    unnamed x41, local copies, waits for them, and re-layouts  19.9 us
    gather x2, local copies, waits for them, and re-layouts, on_device(): jnp.take(flat_source, margin_index, axis=1)  19.2 us
  transfers between devices with their start and end apart: 7, of which 5 were waited for; matrix products, arithmetic and copies ran while one was open for 55% of the time, Pallas kernels for 0%

profile of v1, /device:TPU:0, one launch (start us, length us, event | category | flops | bytes accessed | tf_op | source)
XLA Modules:
  0.0 538.7 jit_solution(11126708305411356537)
XLA Ops:
  7.2 1.7 bitcast_dynamic-update-slice_fusion.7
  15.5 1.7 bitcast_dynamic-update-slice_fusion.2
  18.9 1.7 bitcast_dynamic-update-slice_fusion
  20.6 5.2 all-to-all-start
  26.6 2.9 gather_fusion
  30.1 22.3 %all-to-all-done = bf16[8,64,1,2048]{3,1,2,0:T(8,128)(2,1)S(1)} async-done(((bf16[8,64,1,2048]{3,1,2,0:T(8,128)(2,1)}), bf16[8,64,1,2048]{3,1,2,0:T(8,128)(2,1)S(1)}, u32[]{:S(2)}, u32[]{:S(2)}) %all-to-all-start) | async-done | bytes 2097184 | tf_op jit(solution)/shard_map/all_to_all | solution.py:92
  53.9 116.3 %while.16 = (s32[]{:T(128)}, f32[64,4096]{1,0:T(8,128)}, f32[4096]{0:T(1024)S(1)}, bf16[64,16384]{1,0:T(8,128)(2,1)}, s32[16384]{0:T(1024)S(1)}, /*index=5*/s32[]{:T(128)}, s32[]{:T(128)}, s32[]{:T(128)}, s32[]{:T(128)}) while((s32[]{:T(128)}, f32[64,4096]{1,0:T(8,128)}, f32[4096]{0:T(1024)S(1)}, bf16[64,16384]{1,0:T(8,128)(2,1)}, ...), condition=%wide.region_2.0_spmd.clone, body=%wide.region_0.0_spmd.clone.sunk | while | flops 1116213248 | bytes 2457758 | solution.py:78
  53.9 8.9 %fusion.65 = f32[64,4096]{1,0:T(8,128)} fusion(s32[2048]{0:T(1024)S(1)} %dynamic_slice.29, f32[64,4096]{1,0:T(8,128)} %get-tuple-element.197, pred[]{:T(512)S(6)} %compare.4, bf16[64,16384]{1,0:T(8,128)(2,1)} %get-tuple-element.208, s32[]{:T(128)S(6)} %select_n.172), kind=kOutput, calls=%fused_computation.10.clone.1 | convolution fusion | flops 1082654720 | bytes 2367493 | tf_op jit(solution)/shard_map/while/body/eval_jaxpr/dot_general | solution.py:70
  62.7 5.3 convert_reduce_fusion.2
  68.1 9.2 %fusion.65 = f32[64,4096]{1,0:T(8,128)} fusion(s32[2048]{0:T(1024)S(1)} %dynamic_slice.29, f32[64,4096]{1,0:T(8,128)} %get-tuple-element.197, pred[]{:T(512)S(6)} %compare.4, bf16[64,16384]{1,0:T(8,128)(2,1)} %get-tuple-element.208, s32[]{:T(128)S(6)} %select_n.172), kind=kOutput, calls=%fused_computation.10.clone.1 | convolution fusion | flops 1082654720 | bytes 2367493 | tf_op jit(solution)/shard_map/while/body/eval_jaxpr/dot_general | solution.py:70
  77.3 5.3 convert_reduce_fusion.2
  82.6 9.2 %fusion.65 = f32[64,4096]{1,0:T(8,128)} fusion(s32[2048]{0:T(1024)S(1)} %dynamic_slice.29, f32[64,4096]{1,0:T(8,128)} %get-tuple-element.197, pred[]{:T(512)S(6)} %compare.4, bf16[64,16384]{1,0:T(8,128)(2,1)} %get-tuple-element.208, s32[]{:T(128)S(6)} %select_n.172), kind=kOutput, calls=%fused_computation.10.clone.1 | convolution fusion | flops 1082654720 | bytes 2367493 | tf_op jit(solution)/shard_map/while/body/eval_jaxpr/dot_general | solution.py:70
  91.9 5.3 convert_reduce_fusion.2
  97.2 9.2 %fusion.65 = f32[64,4096]{1,0:T(8,128)} fusion(s32[2048]{0:T(1024)S(1)} %dynamic_slice.29, f32[64,4096]{1,0:T(8,128)} %get-tuple-element.197, pred[]{:T(512)S(6)} %compare.4, bf16[64,16384]{1,0:T(8,128)(2,1)} %get-tuple-element.208, s32[]{:T(128)S(6)} %select_n.172), kind=kOutput, calls=%fused_computation.10.clone.1 | convolution fusion | flops 1082654720 | bytes 2367493 | tf_op jit(solution)/shard_map/while/body/eval_jaxpr/dot_general | solution.py:70
  106.4 5.3 convert_reduce_fusion.2
  111.8 9.2 %fusion.65 = f32[64,4096]{1,0:T(8,128)} fusion(s32[2048]{0:T(1024)S(1)} %dynamic_slice.29, f32[64,4096]{1,0:T(8,128)} %get-tuple-element.197, pred[]{:T(512)S(6)} %compare.4, bf16[64,16384]{1,0:T(8,128)(2,1)} %get-tuple-element.208, s32[]{:T(128)S(6)} %select_n.172), kind=kOutput, calls=%fused_computation.10.clone.1 | convolution fusion | flops 1082654720 | bytes 2367493 | tf_op jit(solution)/shard_map/while/body/eval_jaxpr/dot_general | solution.py:70
  121.0 5.3 convert_reduce_fusion.2
  126.3 9.2 %fusion.65 = f32[64,4096]{1,0:T(8,128)} fusion(s32[2048]{0:T(1024)S(1)} %dynamic_slice.29, f32[64,4096]{1,0:T(8,128)} %get-tuple-element.197, pred[]{:T(512)S(6)} %compare.4, bf16[64,16384]{1,0:T(8,128)(2,1)} %get-tuple-element.208, s32[]{:T(128)S(6)} %select_n.172), kind=kOutput, calls=%fused_computation.10.clone.1 | convolution fusion | flops 1082654720 | bytes 2367493 | tf_op jit(solution)/shard_map/while/body/eval_jaxpr/dot_general | solution.py:70
  135.5 5.3 convert_reduce_fusion.2
  140.9 9.2 %fusion.65 = f32[64,4096]{1,0:T(8,128)} fusion(s32[2048]{0:T(1024)S(1)} %dynamic_slice.29, f32[64,4096]{1,0:T(8,128)} %get-tuple-element.197, pred[]{:T(512)S(6)} %compare.4, bf16[64,16384]{1,0:T(8,128)(2,1)} %get-tuple-element.208, s32[]{:T(128)S(6)} %select_n.172), kind=kOutput, calls=%fused_computation.10.clone.1 | convolution fusion | flops 1082654720 | bytes 2367493 | tf_op jit(solution)/shard_map/while/body/eval_jaxpr/dot_general | solution.py:70
  150.1 5.3 convert_reduce_fusion.2
  155.4 9.2 %fusion.65 = f32[64,4096]{1,0:T(8,128)} fusion(s32[2048]{0:T(1024)S(1)} %dynamic_slice.29, f32[64,4096]{1,0:T(8,128)} %get-tuple-element.197, pred[]{:T(512)S(6)} %compare.4, bf16[64,16384]{1,0:T(8,128)(2,1)} %get-tuple-element.208, s32[]{:T(128)S(6)} %select_n.172), kind=kOutput, calls=%fused_computation.10.clone.1 | convolution fusion | flops 1082654720 | bytes 2367493 | tf_op jit(solution)/shard_map/while/body/eval_jaxpr/dot_general | solution.py:70
  164.7 5.3 convert_reduce_fusion.2
  175.0 2.5 collective-permute-done.1
  177.5 2.1 maximum_maximum_fusion
  179.6 3.9 copy.82
  183.5 17.3 %gather_fusion.1 = bf16[8000,64]{1,0:T(8,128)(2,1)} fusion(bf16[64,12800]{0,1:T(8,128)(2,1)S(1)} %bitcast.92, s32[8192]{0:T(1024)S(1)} %pad_clamp_fusion), kind=kCustom, calls=%fused_computation.1 | custom fusion | bytes 2080000 | tf_op jit(solution)/shard_map/jit(_take)/gather | solution.py:120
  200.8 1.9 copy.85
  203.9 4.8 all-to-all-start.1
  210.6 13.9 %all-reduce.1 = bf16[256]{0:T(256)(128)(2,1)S(1)} all-reduce(bf16[256]{0:T(256)(128)(2,1)S(1)} %dynamic-update-slice), channel_id=1, replica_groups=mesh['space'=8,'chan'=4] {'chan'}, use_global_device_ids=true, to_apply=%add.1 | all-reduce | flops 256 | bytes 1024
  226.0 6.2 %all-to-all-done.1 = bf16[64,8,1000]{2,0,1:T(8,128)(2,1)S(1)} async-done(((bf16[64,8,1000]{2,0,1:T(8,128)(2,1)}), bf16[64,8,1000]{2,0,1:T(8,128)(2,1)S(1)}, u32[]{:S(2)}, u32[]{:S(2)}) %all-to-all-start.1) | async-done | bytes 1024032 | tf_op jit(solution)/shard_map/all_to_all | solution.py:121
  233.1 3.8 copy.94
  238.2 108.8 %gather_fusion.2 = bf16[27648,256]{1,0:T(8,128)(2,1)} fusion(bf16[256,2000]{0,1:T(8,128)(2,1)S(1)} %reshape.270, s32[27648]{0:T(1024)S(1)} %broadcast_clamp_fusion), kind=kCustom, calls=%fused_computation.2 | custom fusion | bytes 28422144 | tf_op jit(solution)/shard_map/jit(_take)/gather | solution.py:127
  347.1 18.6 %copy.88 = bf16[27,1024,256]{1,2,0:T(8,128)(2,1)} copy(bf16[27,1024,256]{2,1,0:T(8,128)(2,1)} %bitcast.91) | data formatting | bytes 28311552 | tf_op jit(solution)/shard_map/jit(_take)/gather | solution.py:127
  365.7 12.6 %select_bitcast_fusion = bf16[256,27,1024]{2,0,1:T(8,128)(2,1)} fusion(bf16[27,1024,256]{1,2,0:T(8,128)(2,1)} %copy.88, pred[27,1024]{1,0:T(8,128)(4,1)S(1)} %compare_and_fusion.1), kind=kLoop, calls=%fused_computation.14 | loop fusion | flops 7077888 | bytes 28339200 | tf_op jit(solution)/shard_map/jit(_take)/select_n | solution.py:127
  378.3 3.6 fusion.40
  381.9 2.8 copy-done
  384.7 2.5 fusion.43
  391.0 7.4 %all-to-all-start.2 = ((bf16[4,64,1024]{2,1,0:T(8,128)(2,1)}), bf16[4,64,1024]{2,1,0:T(8,128)(2,1)S(1)}, u32[]{:S(2)}, u32[]{:S(2)}) async-start(bf16[4,64,1024]{2,1,0:T(8,128)(2,1)} %bitcast.27), calls=%async_computation.2 | async-start | bytes 1048576 | tf_op jit(solution)/shard_map/all_to_all | solution.py:143
  398.4 15.2 %all-to-all-done.2 = bf16[4,64,1024]{2,1,0:T(8,128)(2,1)S(1)} async-done(((bf16[4,64,1024]{2,1,0:T(8,128)(2,1)}), bf16[4,64,1024]{2,1,0:T(8,128)(2,1)S(1)}, u32[]{:S(2)}, u32[]{:S(2)}) %all-to-all-start.2) | async-done | bytes 524320 | tf_op jit(solution)/shard_map/all_to_all | solution.py:143
  414.3 57.4 %gather_fusion.3 = bf16[16384,64]{1,0:T(8,128)(2,1)} fusion(bf16[64,4097]{0,1:T(8,128)(2,1)S(1)} %concatenate.7, s32[16384]{0:T(1024)S(1)} %broadcast_clamp_fusion.1), kind=kCustom, calls=%fused_computation.3 | custom fusion | bytes 4259840 | tf_op jit(solution)/shard_map/jit(_take)/gather | solution.py:145
  471.7 4.8 copy.91
  476.5 3.1 broadcast_select_fusion
  479.6 11.8 %all-to-all-start.3 = ((bf16[64,8,2048]{2,0,1:T(8,128)(2,1)}), bf16[64,8,2048]{2,0,1:T(8,128)(2,1)}, u32[]{:S(2)}, u32[]{:S(2)}) async-start(bf16[64,8,2048]{2,0,1:T(8,128)(2,1)} %broadcast_select_fusion), calls=%async_computation.3 | async-start | bytes 4194304 | tf_op jit(solution)/shard_map/all_to_all | solution.py:146
  492.5 25.6 %all-to-all-done.3 = bf16[64,8,2048]{2,0,1:T(8,128)(2,1)} async-done(((bf16[64,8,2048]{2,0,1:T(8,128)(2,1)}), bf16[64,8,2048]{2,0,1:T(8,128)(2,1)}, u32[]{:S(2)}, u32[]{:S(2)}) %all-to-all-start.3) | async-done | bytes 2097184 | tf_op jit(solution)/shard_map/all_to_all | solution.py:146
  518.1 4.8 copy.92
  522.8 5.1 reshape.227
  528.0 3.9 add_convert_fusion
  (96 shorter events, 27.6 us)
Async XLA Ops:
  15.5 11.0 %copy-start.6 = (s32[8,27]{1,0:T(8,128)S(1)}, s32[8,27]{1,0:T(8,128)}, u32[]{:S(2)}) copy-start(s32[8,27]{1,0:T(8,128)} %param.14) | copy-start | bytes 2596
  15.5 11.1 %copy-start.7 = (s32[1000]{0:T(1024)S(1)}, s32[1000]{0:T(1024)}, u32[]{:S(2)}) copy-start(s32[1000]{0:T(1024)} %constant.140) | copy-start | bytes 12004
  18.9 11.0 %copy-start.5 = (s32[1000]{0:T(1024)S(1)}, s32[1000]{0:T(1024)}, u32[]{:S(2)}) copy-start(s32[1000]{0:T(1024)} %constant.126.clone) | copy-start | bytes 12004
  18.9 11.1 %copy-start.3 = (s32[1,16384]{1,0:T(1,128)S(1)}, s32[1,16384]{1,0:T(1,128)}, u32[]{:S(2)}) copy-start(s32[1,16384]{1,0:T(1,128)} %param.11) | copy-start | bytes 196612
  20.6 31.8 %all-to-all-start = ((bf16[8,64,1,2048]{3,1,2,0:T(8,128)(2,1)}), bf16[8,64,1,2048]{3,1,2,0:T(8,128)(2,1)S(1)}, u32[]{:S(2)}, u32[]{:S(2)}) async-start(bf16[8,64,1,2048]{3,1,2,0:T(8,128)(2,1)} %bitcast_dynamic-update-slice_fusion), calls=%async_computation | async-start | bytes 4194304 | tf_op jit(solution)/shard_map/all_to_all | solution.py:92
  25.8 352.6 %all-gather.2.cloned.1.call-start = ((), (), s32[]{:S(2)}) async-start(), calls=%async_computation.4 | async-start | bytes 4423680 | tf_op jit(solution)/shard_map/all_gather | solution.py:111
  171.6 3.3 collective-permute-start
  173.0 4.5 collective-permute-start.1
  200.8 7.9 %copy-start.4 = (s32[27,512]{1,0:T(8,128)S(1)}, s32[27,512]{1,0:T(8,128)}, u32[]{:S(2)}) copy-start(s32[27,512]{1,0:T(8,128)} %constant.127.clone) | copy-start | bytes 165892
  202.8 6.3 %copy-start.10 = (u32[32]{0:T(128)S(1)}, u32[32]{0:T(128)}, u32[]{:S(2)}) copy-start(u32[32]{0:T(128)} %constant.143) | copy-start | bytes 388
  202.8 7.6 %copy-start.9 = (bf16[64]{0:T(256)(128)(2,1)S(1)}, bf16[64]{0:T(256)(128)(2,1)}, u32[]{:S(2)}) copy-start(bf16[64]{0:T(256)(128)(2,1)} %param.13) | copy-start | bytes 388
  203.9 28.3 %all-to-all-start.1 = ((bf16[64,8,1000]{2,0,1:T(8,128)(2,1)}), bf16[64,8,1000]{2,0,1:T(8,128)(2,1)S(1)}, u32[]{:S(2)}, u32[]{:S(2)}) async-start(bf16[64,8,1000]{2,0,1:T(8,128)(2,1)} %broadcast_select_fusion.1), calls=%async_computation.1 | async-start | bytes 2097152 | tf_op jit(solution)/shard_map/all_to_all | solution.py:121
  232.1 1.0 copy-start.2
  378.3 6.4 %copy-start = (bf16[256,27,1024]{2,0,1:T(8,128)(2,1)S(1)}, bf16[256,27,1024]{2,0,1:T(8,128)(2,1)}, u32[]{:S(2)}) copy-start(bf16[256,27,1024]{2,0,1:T(8,128)(2,1)} %select_bitcast_fusion) | copy-start | bytes 42467332
  384.7 2.5 copy-start.8
  391.0 22.6 %all-to-all-start.2 = ((bf16[4,64,1024]{2,1,0:T(8,128)(2,1)}), bf16[4,64,1024]{2,1,0:T(8,128)(2,1)S(1)}, u32[]{:S(2)}, u32[]{:S(2)}) async-start(bf16[4,64,1024]{2,1,0:T(8,128)(2,1)} %bitcast.27), calls=%async_computation.2 | async-start | bytes 1048576 | tf_op jit(solution)/shard_map/all_to_all | solution.py:143
  479.6 38.5 %all-to-all-start.3 = ((bf16[64,8,2048]{2,0,1:T(8,128)(2,1)}), bf16[64,8,2048]{2,0,1:T(8,128)(2,1)}, u32[]{:S(2)}, u32[]{:S(2)}) async-start(bf16[64,8,2048]{2,0,1:T(8,128)(2,1)} %broadcast_select_fusion), calls=%async_computation.3 | async-start | bytes 4194304 | tf_op jit(solution)/shard_map/all_to_all | solution.py:146
  522.8 5.1 copy-start.1
Sparse Core Ops, SparseCore 0:
  28.2 71.6 all-gather.1
